TPU v7x, 32 devices: a whole 2x2x4 slice. The times are simulated.
32 devices in a mesh: groups: 2 (over y), text: 4 (over z), image: 4 (over x, core).
Axes of the slice: x: 2, y: 2, z: 4, core: 2. Of those that a mesh axis runs over, the one named last changes fastest.
Arguments:
- text_states: bfloat16 [1024, 8192], P(('groups', 'text')), parts along dimension 0, may hold values from -6 to 6
- grid_levels: bfloat16 [16384, 8192], P(('groups', 'text'), 'image'), parts along dimension 0, may hold values from -8 to 7, as said below
- round_logits: float32 [16384, 8192], P(('groups', 'text'), 'image'), parts along dimension 0, may hold values from -2 to 2
- column_steps: float32 [16384], P(('groups', 'image')), parts along dimension 0, may hold values from 0.0015 to 0.004
- image_keys: bfloat16 [12808, 1024], P('groups', 'image'), parts along dimension 0, may hold values from -500 to 500
- image_values: bfloat16 [12808, 1024], P('groups', 'image'), parts along dimension 0, may hold values from -6 to 6
- target_out: bfloat16 [1024, 8192], P(('groups', 'text'), 'image'), parts along dimension 0, may hold values from -6 to 6
- doc_images: int32 [6], P('groups'), parts along dimension 0, may hold values from 1 to 2, as said below
- image_start: int32 [8], P('groups'), parts along dimension 0, may hold values from 1 to 3, as said below
Outputs:
- rounding_grad: float32 [16384, 8192], P(('groups', 'text'), 'image'), parts along dimension 0
There are 2 independent parts, one for each index of `groups`. A program takes and returns all parts, laid end to end along the dimension named above; each array names one. Nothing has to cross between parts.
Inputs may be any that keep to these rules, and one draw needn't show every extreme that they name: `doc_images`: every document holds one image or more, 4 in all; one document holds exactly 2, and no document more. `image_start`: Nondecreasing; the first image's entry is 1 and the last image's 4 - 1. `grid_levels`: whole numbers.
All inputs are finite; a program needn't handle non-finite values.
Results may differ from a plain program's by a relative error of at most 0.015.
Values may be sent and summed in bfloat16 or wider, within the bound.
A program may use at most 256 MiB of HBM per device.

v0:
```python
import jax
import jax.numpy as jnp
from jax import lax
from jax.sharding import PartitionSpec as P

H = 64
KVH = 8
HD = 128
IMAGES = 4
IMG_TOK = 1601
SPAN = 128


def visibility(span_ids, doc_images, image_start, total_spans):
    images = image_start.shape[0]
    documents = doc_images.shape[0]
    doc_ends = jnp.cumsum(doc_images)
    positions = jnp.arange(images, dtype=jnp.int32)
    doc_of = jnp.sum((positions[:, None] >= doc_ends[None, :]).astype(jnp.int32), axis=1)
    doc_index = jnp.arange(documents, dtype=jnp.int32)
    end_of = jnp.sum(jnp.where(doc_index[None, :] == doc_of[:, None], doc_ends[None, :], 0), axis=1)
    stop_at = jnp.sum(
        jnp.where(positions[None, :] == end_of[:, None], image_start[None, :], 0), axis=1
    )
    stop_at = stop_at + jnp.where(end_of >= images, total_spans, 0)
    return (span_ids[:, None] >= image_start[None, :]) & (span_ids[:, None] < stop_at[None, :])


def head_grad(queries, keys, values, target, visible):
    tokens_here = queries.shape[0]
    kv_heads = queries.shape[1]
    per_group = queries.shape[2]
    head_size = queries.shape[3]
    scaling = head_size ** (-0.5)
    shape = (kv_heads, per_group, tokens_here)

    def tile_of(which):
        keys_now = lax.dynamic_slice_in_dim(keys, which * IMG_TOK, IMG_TOK, 0)
        values_now = lax.dynamic_slice_in_dim(values, which * IMG_TOK, IMG_TOK, 0)
        scores = (
            jnp.einsum("tkgd,nkd->kgtn", queries, keys_now, preferred_element_type=jnp.float32)
            * scaling
        )
        return (scores, keys_now, values_now)

    def seen_of(which):
        return lax.dynamic_index_in_dim(visible, which, 1, keepdims=False)

    def forward(which, state):
        seen_rows = seen_of(which)
        running, total, accum = state
        scores, keys_now, values_now = tile_of(which)
        seen = seen_rows[None, None, :]
        peak = jnp.where(seen, jnp.maximum(running, jnp.max(scores, axis=-1)), running)
        weights = jnp.where(seen[..., None], jnp.exp(scores - peak[..., None]), 0.0)
        fade = jnp.exp(running - peak)
        total = total * fade + jnp.sum(weights, axis=-1)
        product = jnp.einsum(
            "kgtn,nkd->kgtd",
            weights.astype(jnp.bfloat16),
            values_now,
            preferred_element_type=jnp.float32,
        )
        return (peak, total, accum * fade[..., None] + product)

    start_state = (
        jnp.full(shape, -1e30, jnp.float32),
        jnp.zeros(shape, jnp.float32),
        jnp.zeros(shape + (head_size,), jnp.float32),
    )
    running, total, accum = lax.fori_loop(0, IMAGES, forward, start_state)
    denom = jnp.maximum(total, 1.0)
    attended = accum / denom[..., None]
    out_grad = (1024.0 * (attended - target)).astype(jnp.bfloat16)
    delta = jnp.sum(out_grad.astype(jnp.float32) * attended, axis=-1)

    def backward(which, grad_acc):
        seen_rows = seen_of(which)
        scores, keys_now, values_now = tile_of(which)
        seen = seen_rows[None, None, :]
        probs = (
            jnp.where(seen[..., None], jnp.exp(scores - running[..., None]), 0.0) / denom[..., None]
        )
        dprob = jnp.einsum(
            "kgtd,nkd->kgtn", out_grad, values_now, preferred_element_type=jnp.float32
        )
        score_grad = (probs * (dprob - delta[..., None]) * scaling).astype(jnp.bfloat16)
        return grad_acc + jnp.einsum(
            "kgtn,nkd->kgtd", score_grad, keys_now, preferred_element_type=jnp.float32
        )

    grad_sum = lax.fori_loop(0, IMAGES, backward, jnp.zeros(shape + (head_size,), jnp.float32))
    return grad_sum.astype(jnp.bfloat16)


def per_device(
    text_states,
    grid_levels,
    round_logits,
    column_steps,
    image_keys,
    image_values,
    target_out,
    doc_images,
    image_start,
):
    tok_dev = text_states.shape[0]
    out_cols = grid_levels.shape[1]
    n_text = lax.axis_size("text")
    per_group = H // KVH
    kvh_dev = image_keys.shape[1] // HD
    sigmoid_v = jax.nn.sigmoid(round_logits)
    soft = 1.2 * sigmoid_v - 0.1
    weight_q = (column_steps[None, :] * (grid_levels.astype(jnp.float32) + soft)).astype(
        jnp.bfloat16
    )
    spread = lax.all_to_all(text_states, "text", split_axis=1, concat_axis=0, tiled=True)
    q_part = jnp.dot(spread, weight_q, preferred_element_type=jnp.float32)
    q_sum = lax.psum_scatter(q_part, "text", scatter_dimension=0, tiled=True)
    queries = q_sum.astype(jnp.bfloat16)
    first_token = lax.axis_index("text") * tok_dev
    span_ids = (first_token + jnp.arange(tok_dev, dtype=jnp.int32)) // SPAN
    visible = visibility(span_ids, doc_images, image_start, n_text * tok_dev // SPAN)
    query_tiles = queries.reshape(tok_dev, kvh_dev, per_group, HD)
    key_tiles = image_keys.reshape(image_keys.shape[0], kvh_dev, HD)
    value_tiles = image_values.reshape(image_values.shape[0], kvh_dev, HD)
    target_tiles = (
        target_out.astype(jnp.float32)
        .reshape(tok_dev, kvh_dev, per_group, HD)
        .transpose(1, 2, 0, 3)
    )
    grads = head_grad(query_tiles, key_tiles, value_tiles, target_tiles, visible)
    query_grad = grads.transpose(2, 0, 1, 3).reshape(tok_dev, out_cols)
    weight_grad = lax.dot_general(
        spread,
        lax.all_gather(query_grad, "text", axis=0, tiled=True),
        (((0,), (0,)), ((), ())),
        preferred_element_type=jnp.float32,
    )
    hprime = 1.2 * sigmoid_v * (1.0 - sigmoid_v)
    centered = 2.0 * soft - 1.0
    return (weight_grad * column_steps[None, :] - 4.0 * centered * centered * centered) * hprime


def solution(mesh):
    placed = (
        P(("groups", "text"), None),
        P(("groups", "text"), "image"),
        P(("groups", "text"), "image"),
        P(("groups", "image")),
        P("groups", "image"),
        P("groups", "image"),
        P(("groups", "text"), "image"),
        P("groups"),
        P("groups"),
    )
    return jax.shard_map(
        per_device,
        mesh=mesh,
        in_specs=placed,
        out_specs=P(("groups", "text"), "image"),
        check_vma=False,
    )
```

profile of v0, /device:TPU:0, one launch (start us, length us, event | category | flops | bytes accessed | tf_op | source)
XLA Modules:
  0.0 431.3 jit_solution(5376205303469265212)
XLA Ops:
  10.6 6.3 %all-to-all-start = ((bf16[128,4,2048]{0,2,1:T(8,128)(2,1)}), bf16[128,4,2048]{0,2,1:T(8,128)(2,1)S(1)}, u32[]{:S(2)}, u32[]{:S(2)}) async-start(bf16[128,4,2048]{0,2,1:T(8,128)(2,1)} %bitcast.134), calls=%async_computation | async-start | bytes 4194304 | tf_op jit(solution)/shard_map/all_to_all | solution.py:117
  16.9 17.6 %copy.62 = f32[2048,2048]{0,1:T(8,128)} copy(f32[2048,2048]{1,0:T(8,128)} %param.15) | data formatting | bytes 33554432 | tf_op args[2]
  34.5 12.3 %copy.61 = bf16[2048,2048]{0,1:T(8,128)(2,1)} copy(bf16[2048,2048]{1,0:T(8,128)(2,1)} %param.14) | data formatting | bytes 16777216 | tf_op args[1]
  46.8 18.3 %all-to-all-done = bf16[128,4,2048]{0,2,1:T(8,128)(2,1)S(1)} async-done(((bf16[128,4,2048]{0,2,1:T(8,128)(2,1)}), bf16[128,4,2048]{0,2,1:T(8,128)(2,1)S(1)}, u32[]{:S(2)}, u32[]{:S(2)}) %all-to-all-start) | async-done | bytes 2097184 | tf_op jit(solution)/shard_map/all_to_all | solution.py:117
  67.8 14.2 %fusion.47 = f32[512,2048]{0,1:T(8,128)} fusion(bf16[512,2048]{1,0:T(8,128)(2,1)} %bitcast.138, bf16[2048,2048]{0,1:T(8,128)(2,1)} %copy.61, f32[2048]{0:T(1024)S(1)} %copy-done.4, f32[2048,2048]{0,1:T(8,128)} %copy.62), kind=kOutput, calls=%fused_computation.54 | convolution fusion | flops 4332716032 | bytes 31465472 | tf_op jit(solution)/shard_map/dot_general | solution.py:118
  82.5 4.3 %copy.65 = bf16[6404,256]{0,1:T(8,128)(2,1)S(1)} copy(bf16[6404,256]{1,0:T(8,128)(2,1)} %param.18) | data formatting | bytes 6557696 | tf_op args[5]
  100.3 57.7 %reduce-scatter.2.cloned.1.call-done = f32[128,2048]{0,1:T(8,128)} async-done(((f32[512,2048]{0,1:T(8,128)}), f32[128,2048]{0,1:T(8,128)}) %reduce-scatter.2.cloned.1.call-update) | async-done | bytes 1048592 | tf_op jit(solution)/shard_map/reduce_scatter | solution.py:119
  159.6 94.7 %while.32 = (s32[]{:T(128)}, f32[2,8,128]{2,1,0:T(8,128)S(1)}, f32[2,8,128]{2,1,0:T(8,128)S(1)}, f32[2,8,128,128]{3,2,1,0:T(8,128)}, pred[128,4]{0,1:T(4,128)(4,...) while((s32[]{:T(128)}, f32[2,8,128]{2,1,0:T(8,128)S(1)}, ...), condition=%wide.region_8.9_spmd.clone, body=%wide.region_5.8_spmd.clone.sunk | while | flops 1712357376 | bytes 52192112 | solution.py:71
  159.6 7.8 %bitcast_reduce_fusion.2 = (f32[2,8,128]{2,1,0:T(8,128)S(1)}, f32[2,1601,128,8]{2,1,3,0:T(8,128)}) fusion(bf16[128,2,8,128]{3,0,2,1:T(8,128)(2,1)S(1)} %get-tuple-element.659, bf16[6404,2,128]{2,0,1:T(8,128)(2,1)} %get-tuple-element.658, s32[]{:T(128)S(6)} %select_n.117), kind=kOutput, calls=%fused_computation.1.clone.1 | convolution fusion | flops 845940736 | bytes 14471172 | tf_op jit(solution)/shard_map/while/body/eval_jaxpr/tkgd,nkd->kgtn/dot_general | solution.py:41
  167.5 7.3 %fusion.77 = f32[2,8,128]{2,1,0:T(8,128)S(1)} fusion(f32[2,1601,128,8]{2,1,3,0:T(8,128)} %get-tuple-element.616, f32[2,8,128]{2,1,0:T(8,128)S(1)} %maximum_select_fusion.2, pred[128]{0:T(512)(128)(4,1)S(1)} %dynamic-slice_bitcast_fusion.4), kind=kLoop, calls=%fused_computation.5.clone.1 | loop fusion | flops 13113344 | bytes 13131904 | tf_op jit(solution)/shard_map/while/body/eval_jaxpr/reduce_sum | solution.py:57
  174.8 7.5 %fusion.79 = f32[2,8,128,128]{3,2,1,0:T(8,128)S(1)} fusion(f32[2,1601,128,8]{2,1,3,0:T(8,128)} %get-tuple-element.616, f32[2,8,128]{2,1,0:T(8,128)S(1)} %maximum_select_fusion.2, pred[128]{0:T(512)(128)(4,1)S(1)} %dynamic-slice_bitcast_fusion.4, f32[2,8,128,128]{3,2,1,0:T(8,128)S(1)} %copy-done.1, bf16[6404,2,128]{2,0,1:T(8,128)(2,1)} %get-tuple-element.660, ...), kind=kOutput, calls=%fused_computation.8.clone.1 | convolution fusion | flops 853286912 | bytes 16109701 | tf_op jit(solution)/shard_map/while/body/eval_jaxpr/kgtn,nkd->kgtd/dot_general | solution.py:58
  183.3 7.8 %bitcast_reduce_fusion.2 = (f32[2,8,128]{2,1,0:T(8,128)S(1)}, f32[2,1601,128,8]{2,1,3,0:T(8,128)}) fusion(bf16[128,2,8,128]{3,0,2,1:T(8,128)(2,1)S(1)} %get-tuple-element.659, bf16[6404,2,128]{2,0,1:T(8,128)(2,1)} %get-tuple-element.658, s32[]{:T(128)S(6)} %select_n.117), kind=kOutput, calls=%fused_computation.1.clone.1 | convolution fusion | flops 845940736 | bytes 14471172 | tf_op jit(solution)/shard_map/while/body/eval_jaxpr/tkgd,nkd->kgtn/dot_general | solution.py:41
  191.1 7.3 %fusion.77 = f32[2,8,128]{2,1,0:T(8,128)S(1)} fusion(f32[2,1601,128,8]{2,1,3,0:T(8,128)} %get-tuple-element.616, f32[2,8,128]{2,1,0:T(8,128)S(1)} %maximum_select_fusion.2, pred[128]{0:T(512)(128)(4,1)S(1)} %dynamic-slice_bitcast_fusion.4), kind=kLoop, calls=%fused_computation.5.clone.1 | loop fusion | flops 13113344 | bytes 13131904 | tf_op jit(solution)/shard_map/while/body/eval_jaxpr/reduce_sum | solution.py:57
  198.5 7.5 %fusion.79 = f32[2,8,128,128]{3,2,1,0:T(8,128)S(1)} fusion(f32[2,1601,128,8]{2,1,3,0:T(8,128)} %get-tuple-element.616, f32[2,8,128]{2,1,0:T(8,128)S(1)} %maximum_select_fusion.2, pred[128]{0:T(512)(128)(4,1)S(1)} %dynamic-slice_bitcast_fusion.4, f32[2,8,128,128]{3,2,1,0:T(8,128)S(1)} %copy-done.1, bf16[6404,2,128]{2,0,1:T(8,128)(2,1)} %get-tuple-element.660, ...), kind=kOutput, calls=%fused_computation.8.clone.1 | convolution fusion | flops 853286912 | bytes 16109701 | tf_op jit(solution)/shard_map/while/body/eval_jaxpr/kgtn,nkd->kgtd/dot_general | solution.py:58
  206.9 7.8 %bitcast_reduce_fusion.2 = (f32[2,8,128]{2,1,0:T(8,128)S(1)}, f32[2,1601,128,8]{2,1,3,0:T(8,128)}) fusion(bf16[128,2,8,128]{3,0,2,1:T(8,128)(2,1)S(1)} %get-tuple-element.659, bf16[6404,2,128]{2,0,1:T(8,128)(2,1)} %get-tuple-element.658, s32[]{:T(128)S(6)} %select_n.117), kind=kOutput, calls=%fused_computation.1.clone.1 | convolution fusion | flops 845940736 | bytes 14471172 | tf_op jit(solution)/shard_map/while/body/eval_jaxpr/tkgd,nkd->kgtn/dot_general | solution.py:41
  214.8 7.3 %fusion.77 = f32[2,8,128]{2,1,0:T(8,128)S(1)} fusion(f32[2,1601,128,8]{2,1,3,0:T(8,128)} %get-tuple-element.616, f32[2,8,128]{2,1,0:T(8,128)S(1)} %maximum_select_fusion.2, pred[128]{0:T(512)(128)(4,1)S(1)} %dynamic-slice_bitcast_fusion.4), kind=kLoop, calls=%fused_computation.5.clone.1 | loop fusion | flops 13113344 | bytes 13131904 | tf_op jit(solution)/shard_map/while/body/eval_jaxpr/reduce_sum | solution.py:57
  222.1 7.5 %fusion.79 = f32[2,8,128,128]{3,2,1,0:T(8,128)S(1)} fusion(f32[2,1601,128,8]{2,1,3,0:T(8,128)} %get-tuple-element.616, f32[2,8,128]{2,1,0:T(8,128)S(1)} %maximum_select_fusion.2, pred[128]{0:T(512)(128)(4,1)S(1)} %dynamic-slice_bitcast_fusion.4, f32[2,8,128,128]{3,2,1,0:T(8,128)S(1)} %copy-done.1, bf16[6404,2,128]{2,0,1:T(8,128)(2,1)} %get-tuple-element.660, ...), kind=kOutput, calls=%fused_computation.8.clone.1 | convolution fusion | flops 853286912 | bytes 16109701 | tf_op jit(solution)/shard_map/while/body/eval_jaxpr/kgtn,nkd->kgtd/dot_general | solution.py:58
  230.6 7.8 %bitcast_reduce_fusion.2 = (f32[2,8,128]{2,1,0:T(8,128)S(1)}, f32[2,1601,128,8]{2,1,3,0:T(8,128)}) fusion(bf16[128,2,8,128]{3,0,2,1:T(8,128)(2,1)S(1)} %get-tuple-element.659, bf16[6404,2,128]{2,0,1:T(8,128)(2,1)} %get-tuple-element.658, s32[]{:T(128)S(6)} %select_n.117), kind=kOutput, calls=%fused_computation.1.clone.1 | convolution fusion | flops 845940736 | bytes 14471172 | tf_op jit(solution)/shard_map/while/body/eval_jaxpr/tkgd,nkd->kgtn/dot_general | solution.py:41
  238.4 7.3 %fusion.77 = f32[2,8,128]{2,1,0:T(8,128)S(1)} fusion(f32[2,1601,128,8]{2,1,3,0:T(8,128)} %get-tuple-element.616, f32[2,8,128]{2,1,0:T(8,128)S(1)} %maximum_select_fusion.2, pred[128]{0:T(512)(128)(4,1)S(1)} %dynamic-slice_bitcast_fusion.4), kind=kLoop, calls=%fused_computation.5.clone.1 | loop fusion | flops 13113344 | bytes 13131904 | tf_op jit(solution)/shard_map/while/body/eval_jaxpr/reduce_sum | solution.py:57
  245.8 7.5 %fusion.79 = f32[2,8,128,128]{3,2,1,0:T(8,128)S(1)} fusion(f32[2,1601,128,8]{2,1,3,0:T(8,128)} %get-tuple-element.616, f32[2,8,128]{2,1,0:T(8,128)S(1)} %maximum_select_fusion.2, pred[128]{0:T(512)(128)(4,1)S(1)} %dynamic-slice_bitcast_fusion.4, f32[2,8,128,128]{3,2,1,0:T(8,128)S(1)} %copy-done.1, bf16[6404,2,128]{2,0,1:T(8,128)(2,1)} %get-tuple-element.660, ...), kind=kOutput, calls=%fused_computation.8.clone.1 | convolution fusion | flops 853286912 | bytes 16109701 | tf_op jit(solution)/shard_map/while/body/eval_jaxpr/kgtn,nkd->kgtd/dot_general | solution.py:58
  256.5 83.1 %while.33 = (s32[]{:T(128)}, f32[2,8,128,128]{3,2,1,0:T(8,128)}, pred[128,4]{0,1:T(4,128)(4,1)S(1)}, bf16[6404,2,128]{2,0,1:T(8,128)(2,1)}, bf16[128,2,8,128]{3,...) while((s32[]{:T(128)}, f32[2,8,128,128]{3,2,1,0:T(8,128)}, ...), condition=%wide.region_11.12_spmd.clone, body=%wide.region_10.11_spmd.clone.sunk | while | flops 2544910336 | bytes 31930436 | solution.py:92
  256.7 7.9 %fusion.85 = f32[2,1601,128,8]{2,1,3,0:T(8,128)} fusion(bf16[128,2,8,128]{3,0,2,1:T(8,128)(2,1)S(1)} %get-tuple-element.697, bf16[6404,2,128]{2,0,1:T(8,128)(2,1)} %get-tuple-element.696, s32[]{:T(128)S(6)} %select_n.119), kind=kOutput, calls=%fused_computation.35.clone.1 | convolution fusion | flops 839385088 | bytes 14462980 | tf_op jit(solution)/shard_map/while/body/eval_jaxpr/tkgd,nkd->kgtn/dot_general | solution.py:41
  264.6 12.7 %fusion.86 = f32[2,8,128,128]{3,2,1,0:T(8,128)} fusion(f32[2,1601,128,8]{2,1,3,0:T(8,128)} %fusion.85, bf16[2,8,128,128]{3,2,1,0:T(8,128)(2,1)S(1)} %get-tuple-element.701, f32[2,8,128]{2,1,0:T(8,128)S(1)} %get-tuple-element.702, f32[2,8,128]{2,1,0:T(8,128)S(1)} %get-tuple-element.699, f32[2,8,128]{2,1,0:T(8,128)S(1)} %get-tuple-element.698, ...), kind=kOutput, calls=%fused_computation.32.clone.1 | convolution fusion | flops 1705525248 | bytes 17467008 | tf_op jit(solution)/shard_map/while/body/eval_jaxpr/kgtn,nkd->kgtd/dot_general | solution.py:88
  277.3 7.7 %fusion.85 = f32[2,1601,128,8]{2,1,3,0:T(8,128)} fusion(bf16[128,2,8,128]{3,0,2,1:T(8,128)(2,1)S(1)} %get-tuple-element.697, bf16[6404,2,128]{2,0,1:T(8,128)(2,1)} %get-tuple-element.696, s32[]{:T(128)S(6)} %select_n.119), kind=kOutput, calls=%fused_computation.35.clone.1 | convolution fusion | flops 839385088 | bytes 14462980 | tf_op jit(solution)/shard_map/while/body/eval_jaxpr/tkgd,nkd->kgtn/dot_general | solution.py:41
  285.1 13.0 %fusion.86 = f32[2,8,128,128]{3,2,1,0:T(8,128)} fusion(f32[2,1601,128,8]{2,1,3,0:T(8,128)} %fusion.85, bf16[2,8,128,128]{3,2,1,0:T(8,128)(2,1)S(1)} %get-tuple-element.701, f32[2,8,128]{2,1,0:T(8,128)S(1)} %get-tuple-element.702, f32[2,8,128]{2,1,0:T(8,128)S(1)} %get-tuple-element.699, f32[2,8,128]{2,1,0:T(8,128)S(1)} %get-tuple-element.698, ...), kind=kOutput, calls=%fused_computation.32.clone.1 | convolution fusion | flops 1705525248 | bytes 17467008 | tf_op jit(solution)/shard_map/while/body/eval_jaxpr/kgtn,nkd->kgtd/dot_general | solution.py:88
  298.1 7.7 %fusion.85 = f32[2,1601,128,8]{2,1,3,0:T(8,128)} fusion(bf16[128,2,8,128]{3,0,2,1:T(8,128)(2,1)S(1)} %get-tuple-element.697, bf16[6404,2,128]{2,0,1:T(8,128)(2,1)} %get-tuple-element.696, s32[]{:T(128)S(6)} %select_n.119), kind=kOutput, calls=%fused_computation.35.clone.1 | convolution fusion | flops 839385088 | bytes 14462980 | tf_op jit(solution)/shard_map/while/body/eval_jaxpr/tkgd,nkd->kgtn/dot_general | solution.py:41
  305.8 13.0 %fusion.86 = f32[2,8,128,128]{3,2,1,0:T(8,128)} fusion(f32[2,1601,128,8]{2,1,3,0:T(8,128)} %fusion.85, bf16[2,8,128,128]{3,2,1,0:T(8,128)(2,1)S(1)} %get-tuple-element.701, f32[2,8,128]{2,1,0:T(8,128)S(1)} %get-tuple-element.702, f32[2,8,128]{2,1,0:T(8,128)S(1)} %get-tuple-element.699, f32[2,8,128]{2,1,0:T(8,128)S(1)} %get-tuple-element.698, ...), kind=kOutput, calls=%fused_computation.32.clone.1 | convolution fusion | flops 1705525248 | bytes 17467008 | tf_op jit(solution)/shard_map/while/body/eval_jaxpr/kgtn,nkd->kgtd/dot_general | solution.py:88
  318.8 7.7 %fusion.85 = f32[2,1601,128,8]{2,1,3,0:T(8,128)} fusion(bf16[128,2,8,128]{3,0,2,1:T(8,128)(2,1)S(1)} %get-tuple-element.697, bf16[6404,2,128]{2,0,1:T(8,128)(2,1)} %get-tuple-element.696, s32[]{:T(128)S(6)} %select_n.119), kind=kOutput, calls=%fused_computation.35.clone.1 | convolution fusion | flops 839385088 | bytes 14462980 | tf_op jit(solution)/shard_map/while/body/eval_jaxpr/tkgd,nkd->kgtn/dot_general | solution.py:41
  326.6 13.0 %fusion.86 = f32[2,8,128,128]{3,2,1,0:T(8,128)} fusion(f32[2,1601,128,8]{2,1,3,0:T(8,128)} %fusion.85, bf16[2,8,128,128]{3,2,1,0:T(8,128)(2,1)S(1)} %get-tuple-element.701, f32[2,8,128]{2,1,0:T(8,128)S(1)} %get-tuple-element.702, f32[2,8,128]{2,1,0:T(8,128)S(1)} %get-tuple-element.699, f32[2,8,128]{2,1,0:T(8,128)S(1)} %get-tuple-element.698, ...), kind=kOutput, calls=%fused_computation.32.clone.1 | convolution fusion | flops 1705525248 | bytes 17467008 | tf_op jit(solution)/shard_map/while/body/eval_jaxpr/kgtn,nkd->kgtd/dot_general | solution.py:88
  341.8 46.9 %all-gather.2.cloned.1.call-done = bf16[512,2048]{0,1:T(8,128)(2,1)} async-done(((bf16[128,2048]{0,1:T(8,128)(2,1)}), bf16[512,2048]{0,1:T(8,128)(2,1)}) %all-gather.2.cloned.1.call-update) | async-done | bytes 2097168 | tf_op jit(solution)/shard_map/all_gather | solution.py:136
  388.7 18.2 %fusion.42 = f32[2048,2048]{0,1:T(8,128)} fusion(bf16[512,2048]{0,1:T(8,128)(2,1)} %all-gather.2.cloned.1.call-done, bf16[512,2048]{1,0:T(8,128)(2,1)S(1)} %bitcast.139, f32[2048]{0:T(1024)S(1)} %copy-done.5, f32[2048,2048]{0,1:T(8,128)} %copy.62), kind=kOutput, calls=%fused_computation.47 | convolution fusion | flops 4357881856 | bytes 37756928 | tf_op jit(solution)/shard_map/dot_general | solution.py:134
  406.9 17.6 %copy.76 = f32[2048,2048]{1,0:T(8,128)} copy(f32[2048,2048]{0,1:T(8,128)} %fusion.42) | data formatting | bytes 33554432 | tf_op jit(solution)/shard_map/mul | solution.py:142
  (74 shorter events, 30.6 us)
Async XLA Ops:
  10.6 54.5 %all-to-all-start = ((bf16[128,4,2048]{0,2,1:T(8,128)(2,1)}), bf16[128,4,2048]{0,2,1:T(8,128)(2,1)S(1)}, u32[]{:S(2)}, u32[]{:S(2)}) async-start(bf16[128,4,2048]{0,2,1:T(8,128)(2,1)} %bitcast.134), calls=%async_computation | async-start | bytes 4194304 | tf_op jit(solution)/shard_map/all_to_all | solution.py:117
  16.9 141.1 %reduce-scatter.2.cloned.1.call-start = ((), (), s32[]{:S(2)}) async-start(), calls=%async_computation.2 | async-start | bytes 5242880 | tf_op jit(solution)/shard_map/reduce_scatter | solution.py:119
  34.5 33.3 %copy-start.4 = (f32[2048]{0:T(1024)S(1)}, f32[2048]{0:T(1024)}, u32[]{:S(2)}) copy-start(f32[2048]{0:T(1024)} %param.16) | copy-start | bytes 24580
  67.8 14.5 %copy-start.6 = (s32[3]{0:T(128)S(1)}, s32[3]{0:T(128)}, u32[]{:S(2)}) copy-start(s32[3]{0:T(128)} %param.20) | copy-start | bytes 40
  82.0 306.7 %all-gather.2.cloned.1.call-start = ((), (), s32[]{:S(2)}) async-start(), calls=%async_computation.3 | async-start | bytes 2621440 | tf_op jit(solution)/shard_map/all_gather | solution.py:136
  82.5 17.5 %copy-start.3 = (s32[4]{0:T(128)S(1)}, s32[4]{0:T(128)}, u32[]{:S(2)}) copy-start(s32[4]{0:T(128)} %param.21) | copy-start | bytes 52
  159.6 15.2 %copy-start.1 = (f32[2,8,128,128]{3,2,1,0:T(8,128)S(1)}, f32[2,8,128,128]{3,2,1,0:T(8,128)}, u32[]{:S(2)}) copy-start(f32[2,8,128,128]{3,2,1,0:T(8,128)} %get-tuple-element.644) | copy-start | bytes 3145732 | tf_op jit(solution)/shard_map/while
  182.3 1.0 copy-start.2
  183.3 15.2 %copy-start.1 = (f32[2,8,128,128]{3,2,1,0:T(8,128)S(1)}, f32[2,8,128,128]{3,2,1,0:T(8,128)}, u32[]{:S(2)}) copy-start(f32[2,8,128,128]{3,2,1,0:T(8,128)} %get-tuple-element.644) | copy-start | bytes 3145732 | tf_op jit(solution)/shard_map/while
  205.9 1.0 copy-start.2
  206.9 15.2 %copy-start.1 = (f32[2,8,128,128]{3,2,1,0:T(8,128)S(1)}, f32[2,8,128,128]{3,2,1,0:T(8,128)}, u32[]{:S(2)}) copy-start(f32[2,8,128,128]{3,2,1,0:T(8,128)} %get-tuple-element.644) | copy-start | bytes 3145732 | tf_op jit(solution)/shard_map/while
  229.6 1.0 copy-start.2
  230.6 15.2 %copy-start.1 = (f32[2,8,128,128]{3,2,1,0:T(8,128)S(1)}, f32[2,8,128,128]{3,2,1,0:T(8,128)}, u32[]{:S(2)}) copy-start(f32[2,8,128,128]{3,2,1,0:T(8,128)} %get-tuple-element.644) | copy-start | bytes 3145732 | tf_op jit(solution)/shard_map/while
  253.3 1.0 copy-start.2
  256.5 132.2 %copy-start = (bf16[4,128,2048]{2,1,0:T(8,128)(2,1)S(1)}, bf16[4,128,2048]{2,1,0:T(8,128)(2,1)}, u32[]{:S(2)}) copy-start(bf16[4,128,2048]{2,1,0:T(8,128)(2,1)} %copy.64) | copy-start | bytes 6291460
  256.5 132.2 %copy-start.5 = (f32[2048]{0:T(1024)S(1)}, f32[2048]{0:T(1024)}, u32[]{:S(2)}) copy-start(f32[2048]{0:T(1024)} %param.16) | copy-start | bytes 24580
Sparse Core Ops, SparseCore 0:
  82.2 75.8 reduce-scatter.1
  341.9 46.7 all-gather.1
where the time goes:
time: 433 us; the launch traced here: 431 us
  matrix products  176 us (41%)
  waiting for transfers between devices  123 us (28%)
  local copies, waits for them, and re-layouts  79.7 us (18%)
  other arithmetic  31.7 us (7%)
  between operations  13.5 us (3%)
  starting transfers between devices  6.54 us (2%)
    dot_general x8, matrix products, tile_of(): jnp.einsum('tkgd,nkd->kgtn', queries, keys_now, preferred_element_type=jn...  62.4 us
    reduce_scatter x1, waiting for transfers between devices, per_device(): q_sum = lax.psum_scatter(q_part, 'text', scatter_dimension=0, tiled=True)  57.7 us
    unnamed x20, local copies, waits for them, and re-layouts  51.7 us
    dot_general x4, matrix products, backward(): jnp.einsum('kgtn,nkd->kgtd', score_grad, keys_now, preferred_element_type...  51.7 us
    all_gather x1, waiting for transfers between devices, per_device(): lax.all_gather(query_grad, 'text', axis=0, tiled=True)  46.9 us
    dot_general x4, matrix products, forward(): jnp.einsum('kgtn,nkd->kgtd', weights.astype(jnp.bfloat16), values_now, pr...  29.9 us
    reduce_sum x4, other arithmetic, forward(): total = total * fade + jnp.sum(weights, axis=-1)  29.2 us
    all_to_all x1, waiting for transfers between devices, per_device(): lax.all_to_all(text_states, 'text', split_axis=1, concat_axis=0, tiled=True)  18.3 us
  transfers between devices with their start and end apart: 3, of which 3 were waited for; matrix products, arithmetic and copies ran while one was open for 11% of the time, Pallas kernels for 0%

commit v1 on v0

--- a/solution.py
+++ b/solution.py
@@ -114,7 +114,12 @@
     weight_q = (column_steps[None, :] * (grid_levels.astype(jnp.float32) + soft)).astype(
         jnp.bfloat16
     )
-    spread = lax.all_to_all(text_states, "text", split_axis=1, concat_axis=0, tiled=True)
+    spread = jnp.concatenate(
+        lax.all_to_all(
+            jnp.stack(jnp.split(text_states, lax.axis_size("text"), axis=1)), "text", 0, 0
+        ),
+        axis=0,
+    )
     q_part = jnp.dot(spread, weight_q, preferred_element_type=jnp.float32)
     q_sum = lax.psum_scatter(q_part, "text", scatter_dimension=0, tiled=True)
     queries = q_sum.astype(jnp.bfloat16)

time: 433 us -> 412 us (0.952)
  blocking collectives: 0 us -> 54.3 us
  local copies, waits for them, and re-layouts: 79.7 us -> 28.3 us
  waiting for transfers between devices: 123 us -> 105 us
  starting transfers between devices: 6.54 us -> 0.22 us
    all_to_all x0 -> x1, blocking collectives: none -> 54.3 us  [per_device(): lax.all_to_all(jnp.stack(jnp.split(text_states, lax.axis_size('text'), ax...]
    unnamed x20 -> x18, local copies, waits for them, and re-layouts: 51.7 us -> 19 us
    all_to_all x1 -> x0, waiting for transfers between devices: 18.3 us -> none  [per_device(): lax.all_to_all(text_states, 'text', split_axis=1, concat_axis=0, tiled=True)]
    mul x1 -> x0, local copies, waits for them, and re-layouts: 17.6 us -> none  [per_device(): (weight_grad * column_steps[None, :] - 4.0 * centered * centered * center...]
    all_to_all x1 -> x0, starting transfers between devices: 6.32 us -> none  [per_device(): lax.all_to_all(text_states, 'text', split_axis=1, concat_axis=0, tiled=True)]
  transfers between devices with their start and end apart: 3 -> 2, of which waited for: 3 -> 2; matrix products, arithmetic and copies ran while one was open for 11% -> 4% of each run, Pallas kernels for 0% -> 0%
where the time goes in v1:
time: 412 us; the launch traced here: 411 us
  matrix products  177 us (43%)
  waiting for transfers between devices  105 us (25%)
  blocking collectives  54.3 us (13%)
  other arithmetic  32 us (8%)
  local copies, waits for them, and re-layouts  28.3 us (7%)
  between operations  13.6 us (3%)
    dot_general x8, matrix products, tile_of(): jnp.einsum('tkgd,nkd->kgtn', queries, keys_now, preferred_element_type=jn...  64.7 us
    reduce_scatter x1, waiting for transfers between devices, per_device(): q_sum = lax.psum_scatter(q_part, 'text', scatter_dimension=0, tiled=True)  58 us
    all_to_all x1, blocking collectives, per_device(): lax.all_to_all(jnp.stack(jnp.split(text_states, lax.axis_size('text'), ax...  54.3 us
    dot_general x4, matrix products, backward(): jnp.einsum('kgtn,nkd->kgtd', score_grad, keys_now, preferred_element_type...  51.9 us
    all_gather x1, waiting for transfers between devices, per_device(): lax.all_gather(query_grad, 'text', axis=0, tiled=True)  46.9 us
    dot_general x4, matrix products, forward(): jnp.einsum('kgtn,nkd->kgtd', weights.astype(jnp.bfloat16), values_now, pr...  29.9 us
    reduce_sum x4, other arithmetic, forward(): total = total * fade + jnp.sum(weights, axis=-1)  29.2 us
    unnamed x18, local copies, waits for them, and re-layouts  19 us
  transfers between devices with their start and end apart: 2, of which 2 were waited for; matrix products, arithmetic and copies ran while one was open for 4% of the time, Pallas kernels for 0%

profile of v1, /device:TPU:0, one launch (start us, length us, event | category | flops | bytes accessed | tf_op | source)
XLA Modules:
  0.0 411.3 jit_solution(1396605471433280631)
XLA Ops:
  8.5 54.3 %all_to_all.5 = bf16[4,128,2048]{2,1,0:T(8,128)(2,1)S(1)} all-to-all(bf16[4,128,2048]{2,1,0:T(8,128)(2,1)S(1)} %pad_maximum_fusion), channel_id=1, replica_groups=mesh['groups'=2,'text'=4,'image'=4] {'text'}, dimensions={0} | all-to-all | bytes 4194304 | tf_op jit(solution)/shard_map/all_to_all | solution.py:118
  64.1 13.3 %fusion.43 = f32[512,2048]{1,0:T(8,128)} fusion(bf16[512,2048]{1,0:T(8,128)(2,1)S(1)} %bitcast.140, bf16[2048,2048]{1,0:T(8,128)(2,1)} %param.14, f32[2048]{0:T(1024)} %param.16, f32[2048,2048]{1,0:T(8,128)} %param.15), kind=kOutput, calls=%fused_computation.50 | convolution fusion | flops 4332716032 | bytes 31465472 | tf_op jit(solution)/shard_map/dot_general | solution.py:123
  78.0 4.3 %copy.31 = bf16[6404,256]{0,1:T(8,128)(2,1)S(1)} copy(bf16[6404,256]{1,0:T(8,128)(2,1)} %param.18) | data formatting | bytes 6557696 | tf_op args[5]
  82.3 3.6 copy.34
  85.9 4.3 %copy.30 = bf16[6404,256]{0,1:T(8,128)(2,1)S(1)} copy(bf16[6404,256]{1,0:T(8,128)(2,1)} %param.17) | data formatting | bytes 6557696 | tf_op args[4]
  90.2 3.6 copy.37
  95.7 58.0 %reduce-scatter.2.cloned.1.call-done = f32[128,2048]{1,0:T(8,128)} async-done(((f32[512,2048]{1,0:T(8,128)}), f32[128,2048]{1,0:T(8,128)}) %reduce-scatter.2.cloned.1.call-update) | async-done | bytes 1048592 | tf_op jit(solution)/shard_map/reduce_scatter | solution.py:124
  155.3 95.8 %while.32 = (s32[]{:T(128)}, f32[2,8,128]{2,1,0:T(8,128)S(1)}, f32[2,8,128]{2,1,0:T(8,128)S(1)}, f32[2,8,128,128]{3,2,1,0:T(8,128)}, pred[128,4]{0,1:T(4,128)(4,...) while((s32[]{:T(128)}, f32[2,8,128]{2,1,0:T(8,128)S(1)}, ...), condition=%wide.region_8.9_spmd.clone, body=%wide.region_5.8_spmd.clone.sunk | while | flops 1712357376 | bytes 52192112 | solution.py:71
  155.3 8.1 %bitcast_reduce_fusion.2 = (f32[2,8,128]{2,1,0:T(8,128)S(1)}, f32[2,1601,128,8]{2,1,3,0:T(8,128)}) fusion(bf16[128,2,8,128]{3,0,2,1:T(8,128)(2,1)S(1)} %get-tuple-element.635, bf16[6404,2,128]{2,0,1:T(8,128)(2,1)} %get-tuple-element.634, s32[]{:T(128)S(6)} %select_n.117), kind=kOutput, calls=%fused_computation.1.clone.1 | convolution fusion | flops 845940736 | bytes 14471172 | tf_op jit(solution)/shard_map/while/body/eval_jaxpr/tkgd,nkd->kgtn/dot_general | solution.py:41
  163.4 7.3 %fusion.76 = f32[2,8,128]{2,1,0:T(8,128)S(1)} fusion(f32[2,1601,128,8]{2,1,3,0:T(8,128)} %get-tuple-element.592, f32[2,8,128]{2,1,0:T(8,128)S(1)} %maximum_select_fusion.2, pred[128]{0:T(512)(128)(4,1)S(1)} %dynamic-slice_bitcast_fusion.4), kind=kLoop, calls=%fused_computation.5.clone.1 | loop fusion | flops 13113344 | bytes 13131904 | tf_op jit(solution)/shard_map/while/body/eval_jaxpr/reduce_sum | solution.py:57
  170.8 7.5 %fusion.78 = f32[2,8,128,128]{3,2,1,0:T(8,128)S(1)} fusion(f32[2,1601,128,8]{2,1,3,0:T(8,128)} %get-tuple-element.592, f32[2,8,128]{2,1,0:T(8,128)S(1)} %maximum_select_fusion.2, pred[128]{0:T(512)(128)(4,1)S(1)} %dynamic-slice_bitcast_fusion.4, f32[2,8,128,128]{3,2,1,0:T(8,128)S(1)} %copy-done.2, bf16[6404,2,128]{2,0,1:T(8,128)(2,1)} %get-tuple-element.636, ...), kind=kOutput, calls=%fused_computation.8.clone.1 | convolution fusion | flops 853286912 | bytes 16109701 | tf_op jit(solution)/shard_map/while/body/eval_jaxpr/kgtn,nkd->kgtd/dot_general | solution.py:58
  179.2 8.1 %bitcast_reduce_fusion.2 = (f32[2,8,128]{2,1,0:T(8,128)S(1)}, f32[2,1601,128,8]{2,1,3,0:T(8,128)}) fusion(bf16[128,2,8,128]{3,0,2,1:T(8,128)(2,1)S(1)} %get-tuple-element.635, bf16[6404,2,128]{2,0,1:T(8,128)(2,1)} %get-tuple-element.634, s32[]{:T(128)S(6)} %select_n.117), kind=kOutput, calls=%fused_computation.1.clone.1 | convolution fusion | flops 845940736 | bytes 14471172 | tf_op jit(solution)/shard_map/while/body/eval_jaxpr/tkgd,nkd->kgtn/dot_general | solution.py:41
  187.3 7.3 %fusion.76 = f32[2,8,128]{2,1,0:T(8,128)S(1)} fusion(f32[2,1601,128,8]{2,1,3,0:T(8,128)} %get-tuple-element.592, f32[2,8,128]{2,1,0:T(8,128)S(1)} %maximum_select_fusion.2, pred[128]{0:T(512)(128)(4,1)S(1)} %dynamic-slice_bitcast_fusion.4), kind=kLoop, calls=%fused_computation.5.clone.1 | loop fusion | flops 13113344 | bytes 13131904 | tf_op jit(solution)/shard_map/while/body/eval_jaxpr/reduce_sum | solution.py:57
  194.7 7.5 %fusion.78 = f32[2,8,128,128]{3,2,1,0:T(8,128)S(1)} fusion(f32[2,1601,128,8]{2,1,3,0:T(8,128)} %get-tuple-element.592, f32[2,8,128]{2,1,0:T(8,128)S(1)} %maximum_select_fusion.2, pred[128]{0:T(512)(128)(4,1)S(1)} %dynamic-slice_bitcast_fusion.4, f32[2,8,128,128]{3,2,1,0:T(8,128)S(1)} %copy-done.2, bf16[6404,2,128]{2,0,1:T(8,128)(2,1)} %get-tuple-element.636, ...), kind=kOutput, calls=%fused_computation.8.clone.1 | convolution fusion | flops 853286912 | bytes 16109701 | tf_op jit(solution)/shard_map/while/body/eval_jaxpr/kgtn,nkd->kgtd/dot_general | solution.py:58
  203.2 8.1 %bitcast_reduce_fusion.2 = (f32[2,8,128]{2,1,0:T(8,128)S(1)}, f32[2,1601,128,8]{2,1,3,0:T(8,128)}) fusion(bf16[128,2,8,128]{3,0,2,1:T(8,128)(2,1)S(1)} %get-tuple-element.635, bf16[6404,2,128]{2,0,1:T(8,128)(2,1)} %get-tuple-element.634, s32[]{:T(128)S(6)} %select_n.117), kind=kOutput, calls=%fused_computation.1.clone.1 | convolution fusion | flops 845940736 | bytes 14471172 | tf_op jit(solution)/shard_map/while/body/eval_jaxpr/tkgd,nkd->kgtn/dot_general | solution.py:41
  211.3 7.3 %fusion.76 = f32[2,8,128]{2,1,0:T(8,128)S(1)} fusion(f32[2,1601,128,8]{2,1,3,0:T(8,128)} %get-tuple-element.592, f32[2,8,128]{2,1,0:T(8,128)S(1)} %maximum_select_fusion.2, pred[128]{0:T(512)(128)(4,1)S(1)} %dynamic-slice_bitcast_fusion.4), kind=kLoop, calls=%fused_computation.5.clone.1 | loop fusion | flops 13113344 | bytes 13131904 | tf_op jit(solution)/shard_map/while/body/eval_jaxpr/reduce_sum | solution.py:57
  218.6 7.5 %fusion.78 = f32[2,8,128,128]{3,2,1,0:T(8,128)S(1)} fusion(f32[2,1601,128,8]{2,1,3,0:T(8,128)} %get-tuple-element.592, f32[2,8,128]{2,1,0:T(8,128)S(1)} %maximum_select_fusion.2, pred[128]{0:T(512)(128)(4,1)S(1)} %dynamic-slice_bitcast_fusion.4, f32[2,8,128,128]{3,2,1,0:T(8,128)S(1)} %copy-done.2, bf16[6404,2,128]{2,0,1:T(8,128)(2,1)} %get-tuple-element.636, ...), kind=kOutput, calls=%fused_computation.8.clone.1 | convolution fusion | flops 853286912 | bytes 16109701 | tf_op jit(solution)/shard_map/while/body/eval_jaxpr/kgtn,nkd->kgtd/dot_general | solution.py:58
  227.1 8.1 %bitcast_reduce_fusion.2 = (f32[2,8,128]{2,1,0:T(8,128)S(1)}, f32[2,1601,128,8]{2,1,3,0:T(8,128)}) fusion(bf16[128,2,8,128]{3,0,2,1:T(8,128)(2,1)S(1)} %get-tuple-element.635, bf16[6404,2,128]{2,0,1:T(8,128)(2,1)} %get-tuple-element.634, s32[]{:T(128)S(6)} %select_n.117), kind=kOutput, calls=%fused_computation.1.clone.1 | convolution fusion | flops 845940736 | bytes 14471172 | tf_op jit(solution)/shard_map/while/body/eval_jaxpr/tkgd,nkd->kgtn/dot_general | solution.py:41
  235.2 7.3 %fusion.76 = f32[2,8,128]{2,1,0:T(8,128)S(1)} fusion(f32[2,1601,128,8]{2,1,3,0:T(8,128)} %get-tuple-element.592, f32[2,8,128]{2,1,0:T(8,128)S(1)} %maximum_select_fusion.2, pred[128]{0:T(512)(128)(4,1)S(1)} %dynamic-slice_bitcast_fusion.4), kind=kLoop, calls=%fused_computation.5.clone.1 | loop fusion | flops 13113344 | bytes 13131904 | tf_op jit(solution)/shard_map/while/body/eval_jaxpr/reduce_sum | solution.py:57
  242.6 7.5 %fusion.78 = f32[2,8,128,128]{3,2,1,0:T(8,128)S(1)} fusion(f32[2,1601,128,8]{2,1,3,0:T(8,128)} %get-tuple-element.592, f32[2,8,128]{2,1,0:T(8,128)S(1)} %maximum_select_fusion.2, pred[128]{0:T(512)(128)(4,1)S(1)} %dynamic-slice_bitcast_fusion.4, f32[2,8,128,128]{3,2,1,0:T(8,128)S(1)} %copy-done.2, bf16[6404,2,128]{2,0,1:T(8,128)(2,1)} %get-tuple-element.636, ...), kind=kOutput, calls=%fused_computation.8.clone.1 | convolution fusion | flops 853286912 | bytes 16109701 | tf_op jit(solution)/shard_map/while/body/eval_jaxpr/kgtn,nkd->kgtd/dot_general | solution.py:58
  253.3 84.5 %while.33 = (s32[]{:T(128)}, f32[2,8,128,128]{3,2,1,0:T(8,128)}, pred[128,4]{0,1:T(4,128)(4,1)S(1)}, bf16[6404,2,128]{2,0,1:T(8,128)(2,1)}, bf16[128,2,8,128]{3,...) while((s32[]{:T(128)}, f32[2,8,128,128]{3,2,1,0:T(8,128)}, ...), condition=%wide.region_11.12_spmd.clone, body=%wide.region_10.11_spmd.clone.sunk | while | flops 2544910336 | bytes 31930436 | solution.py:92
  253.5 8.2 %fusion.84 = f32[2,1601,128,8]{2,1,3,0:T(8,128)} fusion(bf16[128,2,8,128]{3,0,2,1:T(8,128)(2,1)S(1)} %get-tuple-element.673, bf16[6404,2,128]{2,0,1:T(8,128)(2,1)} %get-tuple-element.672, s32[]{:T(128)S(6)} %select_n.119), kind=kOutput, calls=%fused_computation.35.clone.1 | convolution fusion | flops 839385088 | bytes 14462980 | tf_op jit(solution)/shard_map/while/body/eval_jaxpr/tkgd,nkd->kgtn/dot_general | solution.py:41
  261.7 12.8 %fusion.85 = f32[2,8,128,128]{3,2,1,0:T(8,128)} fusion(f32[2,1601,128,8]{2,1,3,0:T(8,128)} %fusion.84, bf16[2,8,128,128]{3,2,1,0:T(8,128)(2,1)S(1)} %get-tuple-element.677, f32[2,8,128]{2,1,0:T(8,128)S(1)} %get-tuple-element.678, f32[2,8,128]{2,1,0:T(8,128)S(1)} %get-tuple-element.675, f32[2,8,128]{2,1,0:T(8,128)S(1)} %get-tuple-element.674, ...), kind=kOutput, calls=%fused_computation.32.clone.1 | convolution fusion | flops 1705525248 | bytes 17467008 | tf_op jit(solution)/shard_map/while/body/eval_jaxpr/kgtn,nkd->kgtd/dot_general | solution.py:88
  274.4 8.0 %fusion.84 = f32[2,1601,128,8]{2,1,3,0:T(8,128)} fusion(bf16[128,2,8,128]{3,0,2,1:T(8,128)(2,1)S(1)} %get-tuple-element.673, bf16[6404,2,128]{2,0,1:T(8,128)(2,1)} %get-tuple-element.672, s32[]{:T(128)S(6)} %select_n.119), kind=kOutput, calls=%fused_computation.35.clone.1 | convolution fusion | flops 839385088 | bytes 14462980 | tf_op jit(solution)/shard_map/while/body/eval_jaxpr/tkgd,nkd->kgtn/dot_general | solution.py:41
  282.5 13.1 %fusion.85 = f32[2,8,128,128]{3,2,1,0:T(8,128)} fusion(f32[2,1601,128,8]{2,1,3,0:T(8,128)} %fusion.84, bf16[2,8,128,128]{3,2,1,0:T(8,128)(2,1)S(1)} %get-tuple-element.677, f32[2,8,128]{2,1,0:T(8,128)S(1)} %get-tuple-element.678, f32[2,8,128]{2,1,0:T(8,128)S(1)} %get-tuple-element.675, f32[2,8,128]{2,1,0:T(8,128)S(1)} %get-tuple-element.674, ...), kind=kOutput, calls=%fused_computation.32.clone.1 | convolution fusion | flops 1705525248 | bytes 17467008 | tf_op jit(solution)/shard_map/while/body/eval_jaxpr/kgtn,nkd->kgtd/dot_general | solution.py:88
  295.5 8.0 %fusion.84 = f32[2,1601,128,8]{2,1,3,0:T(8,128)} fusion(bf16[128,2,8,128]{3,0,2,1:T(8,128)(2,1)S(1)} %get-tuple-element.673, bf16[6404,2,128]{2,0,1:T(8,128)(2,1)} %get-tuple-element.672, s32[]{:T(128)S(6)} %select_n.119), kind=kOutput, calls=%fused_computation.35.clone.1 | convolution fusion | flops 839385088 | bytes 14462980 | tf_op jit(solution)/shard_map/while/body/eval_jaxpr/tkgd,nkd->kgtn/dot_general | solution.py:41
  303.6 13.1 %fusion.85 = f32[2,8,128,128]{3,2,1,0:T(8,128)} fusion(f32[2,1601,128,8]{2,1,3,0:T(8,128)} %fusion.84, bf16[2,8,128,128]{3,2,1,0:T(8,128)(2,1)S(1)} %get-tuple-element.677, f32[2,8,128]{2,1,0:T(8,128)S(1)} %get-tuple-element.678, f32[2,8,128]{2,1,0:T(8,128)S(1)} %get-tuple-element.675, f32[2,8,128]{2,1,0:T(8,128)S(1)} %get-tuple-element.674, ...), kind=kOutput, calls=%fused_computation.32.clone.1 | convolution fusion | flops 1705525248 | bytes 17467008 | tf_op jit(solution)/shard_map/while/body/eval_jaxpr/kgtn,nkd->kgtd/dot_general | solution.py:88
  316.6 8.0 %fusion.84 = f32[2,1601,128,8]{2,1,3,0:T(8,128)} fusion(bf16[128,2,8,128]{3,0,2,1:T(8,128)(2,1)S(1)} %get-tuple-element.673, bf16[6404,2,128]{2,0,1:T(8,128)(2,1)} %get-tuple-element.672, s32[]{:T(128)S(6)} %select_n.119), kind=kOutput, calls=%fused_computation.35.clone.1 | convolution fusion | flops 839385088 | bytes 14462980 | tf_op jit(solution)/shard_map/while/body/eval_jaxpr/tkgd,nkd->kgtn/dot_general | solution.py:41
  324.7 13.1 %fusion.85 = f32[2,8,128,128]{3,2,1,0:T(8,128)} fusion(f32[2,1601,128,8]{2,1,3,0:T(8,128)} %fusion.84, bf16[2,8,128,128]{3,2,1,0:T(8,128)(2,1)S(1)} %get-tuple-element.677, f32[2,8,128]{2,1,0:T(8,128)S(1)} %get-tuple-element.678, f32[2,8,128]{2,1,0:T(8,128)S(1)} %get-tuple-element.675, f32[2,8,128]{2,1,0:T(8,128)S(1)} %get-tuple-element.674, ...), kind=kOutput, calls=%fused_computation.32.clone.1 | convolution fusion | flops 1705525248 | bytes 17467008 | tf_op jit(solution)/shard_map/while/body/eval_jaxpr/kgtn,nkd->kgtd/dot_general | solution.py:88
  337.7 2.2 copy.41
  340.0 46.9 %all-gather.2.cloned.1.call-done = bf16[512,2048]{0,1:T(8,128)(2,1)} async-done(((bf16[128,2048]{0,1:T(8,128)(2,1)}), bf16[512,2048]{0,1:T(8,128)(2,1)}) %all-gather.2.cloned.1.call-update) | async-done | bytes 2097168 | tf_op jit(solution)/shard_map/all_gather | solution.py:141
  386.9 17.6 %fusion.42 = f32[2048,2048]{1,0:T(8,128)} fusion(bf16[512,2048]{1,0:T(8,128)(2,1)S(1)} %bitcast.141, bf16[512,2048]{0,1:T(8,128)(2,1)} %all-gather.2.cloned.1.call-done, f32[2048]{0:T(1024)S(1)} %copy-done.5, f32[2048,2048]{1,0:T(8,128)} %param.15), kind=kOutput, calls=%fused_computation.47 | convolution fusion | flops 4357881856 | bytes 37756928 | tf_op jit(solution)/shard_map/dot_general | solution.py:139
  (71 shorter events, 13.4 us)
Async XLA Ops:
  6.5 147.1 %reduce-scatter.2.cloned.1.call-start = ((), (), s32[]{:S(2)}) async-start(), calls=%async_computation.2 | async-start | bytes 5242880 | tf_op jit(solution)/shard_map/reduce_scatter | solution.py:124
  62.8 1.4 copy-start
  64.1 13.6 %copy-start.6 = (s32[3]{0:T(128)S(1)}, s32[3]{0:T(128)}, u32[]{:S(2)}) copy-start(s32[3]{0:T(128)} %param.20) | copy-start | bytes 40
  77.5 309.4 %all-gather.2.cloned.1.call-start = ((), (), s32[]{:S(2)}) async-start(), calls=%async_computation.3 | async-start | bytes 2621440 | tf_op jit(solution)/shard_map/all_gather | solution.py:141
  78.0 17.4 %copy-start.4 = (s32[4]{0:T(128)S(1)}, s32[4]{0:T(128)}, u32[]{:S(2)}) copy-start(s32[4]{0:T(128)} %param.21) | copy-start | bytes 52
  155.3 15.5 %copy-start.2 = (f32[2,8,128,128]{3,2,1,0:T(8,128)S(1)}, f32[2,8,128,128]{3,2,1,0:T(8,128)}, u32[]{:S(2)}) copy-start(f32[2,8,128,128]{3,2,1,0:T(8,128)} %get-tuple-element.620) | copy-start | bytes 3145732 | tf_op jit(solution)/shard_map/while
  178.2 1.0 copy-start.3
  179.2 15.5 %copy-start.2 = (f32[2,8,128,128]{3,2,1,0:T(8,128)S(1)}, f32[2,8,128,128]{3,2,1,0:T(8,128)}, u32[]{:S(2)}) copy-start(f32[2,8,128,128]{3,2,1,0:T(8,128)} %get-tuple-element.620) | copy-start | bytes 3145732 | tf_op jit(solution)/shard_map/while
  202.2 1.0 copy-start.3
  203.2 15.5 %copy-start.2 = (f32[2,8,128,128]{3,2,1,0:T(8,128)S(1)}, f32[2,8,128,128]{3,2,1,0:T(8,128)}, u32[]{:S(2)}) copy-start(f32[2,8,128,128]{3,2,1,0:T(8,128)} %get-tuple-element.620) | copy-start | bytes 3145732 | tf_op jit(solution)/shard_map/while
  226.1 1.0 copy-start.3
  227.1 15.5 %copy-start.2 = (f32[2,8,128,128]{3,2,1,0:T(8,128)S(1)}, f32[2,8,128,128]{3,2,1,0:T(8,128)}, u32[]{:S(2)}) copy-start(f32[2,8,128,128]{3,2,1,0:T(8,128)} %get-tuple-element.620) | copy-start | bytes 3145732 | tf_op jit(solution)/shard_map/while
  250.0 1.0 copy-start.3
  253.2 133.6 %copy-start.1 = (bf16[4,128,2048]{2,1,0:T(8,128)(2,1)S(1)}, bf16[4,128,2048]{2,1,0:T(8,128)(2,1)}, u32[]{:S(2)}) copy-start(bf16[4,128,2048]{2,1,0:T(8,128)(2,1)} %copy-done) | copy-start | bytes 6291460
  253.3 133.6 %copy-start.5 = (f32[2048]{0:T(1024)S(1)}, f32[2048]{0:T(1024)}, u32[]{:S(2)}) copy-start(f32[2048]{0:T(1024)} %param.16) | copy-start | bytes 24580
Sparse Core Ops, SparseCore 0:
  77.6 75.9 reduce-scatter.1
  340.1 46.6 all-gather.1
